TPU v7x, 512 devices: a whole 4x8x8 slice. The times are simulated.
512 devices in a mesh: user: 8 (over z), item: 4 (over x), tm: 16 (over y, core).
Axes of the slice: x: 4, y: 8, z: 8, core: 2. Of those that a mesh axis runs over, the one named last changes fastest.
Arguments:
- blocks: bfloat16 [8, 4, 16, 8, 64, 4096], P('user', 'item', 'tm'), may hold values from 0 to 8
- block_coords: int32 [8, 4, 16, 8, 3], P('user', 'item', 'tm'), may hold values from 0 to 127, as said below
- block_count: int32 [8, 4, 16], P('user', 'item', 'tm'), may hold values from 1 to 8, as said below
- a_factor: float32 [8192, 128], P(('user', 'item', 'tm')), as said below
- item_factor: bfloat16 [4096, 128], P(('item', 'user', 'tm')), as said below
- hour_factor: bfloat16 [8192, 128], P(('tm', 'user', 'item')), as said below
Outputs:
- new_factor: float32 [8192, 128], P(('user', 'item', 'tm'))
Inputs may be any that keep to these rules, and one draw needn't show every extreme that they name: `block_coords`: the user block of a slot of device (u, i, t) lies in u * 16 to u * 16 + 15, its item block in i * 16 to i * 16 + 15, its hour block in t * 8 to t * 8 + 7; the 8 slots of a device name distinct blocks; slots at or past the device's count are not part of the tensor. `block_count`: some device lists all 8 slots. `a_factor`: entries are nonnegative. `item_factor`: entries are positive. `hour_factor`: entries are positive.
All inputs are finite; a program needn't handle non-finite values.
Results may differ from a plain program's by a relative error of at most 0.00045.
Values may be sent and summed in bfloat16 or wider, within the bound.
A program may use at most 64 MiB of HBM per device.

v0:
```python
import jax
import jax.numpy as jnp
from jax import lax
from jax.sharding import PartitionSpec as P


def update_column(factor, mttkrp, gram, column):
    weights = lax.dynamic_index_in_dim(gram, column, 1, keepdims=False)
    pivot = lax.dynamic_index_in_dim(weights, column, 0, keepdims=False)
    current = lax.dynamic_index_in_dim(factor, column, 1, keepdims=False)
    target = lax.dynamic_index_in_dim(mttkrp, column, 1, keepdims=False)
    fitted = jnp.dot(factor, weights, precision=lax.Precision.HIGHEST)
    fresh = jnp.maximum(current + (target - fitted) / pivot, 0.0)
    return lax.dynamic_update_index_in_dim(factor, fresh, column, 1)


def self_product(matrix):
    return lax.dot_general(
        matrix, matrix, (((0,), (0,)), ((), ())), preferred_element_type=jnp.float32
    )


def per_device(blocks, block_coords, block_count, a_factor, item_factor, hour_factor):
    tiles = blocks.reshape(blocks.shape[3:])
    coords = block_coords.reshape(block_coords.shape[3:])
    count = block_count.reshape(())
    width = tiles.shape[1]
    rank = item_factor.shape[1]
    item_slab = lax.all_gather(item_factor, ("user", "tm"), axis=0, tiled=True)
    hour_slab = lax.all_gather(hour_factor, ("user", "item"), axis=0, tiled=True)
    hour_blocks = hour_slab.reshape(hour_slab.shape[0] // width, width, rank)
    share_rows = a_factor.shape[0]
    user_rows = share_rows * lax.axis_size("item") * lax.axis_size("tm")
    user_first = lax.axis_index("user") * (user_rows // width)
    item_first = lax.axis_index("item") * (item_slab.shape[0] // width)
    hour_first = lax.axis_index("tm") * hour_blocks.shape[0]

    def add_block(totals, tile, coord, hour_rows):
        item_rows = lax.dynamic_slice_in_dim(
            item_slab, (coord[1] - item_first) * width, width, 0
        ).astype(jnp.float32)
        khatri = (
            (item_rows[:, None, :] * hour_rows.astype(jnp.float32)[None, :, :])
            .reshape(width * width, rank)
            .astype(jnp.bfloat16)
        )
        term = jnp.dot(tile, khatri, preferred_element_type=jnp.float32)
        start = (coord[0] - user_first) * width
        current = lax.dynamic_slice_in_dim(totals, start, width, 0)
        return lax.dynamic_update_slice_in_dim(totals, current + term, start, 0)

    def own_step(slot, totals):
        tile = lax.dynamic_index_in_dim(tiles, slot, 0, keepdims=False)
        coord = lax.dynamic_index_in_dim(coords, slot, 0, keepdims=False)
        hour_rows = lax.dynamic_index_in_dim(hour_blocks, coord[2] - hour_first, 0, keepdims=False)
        return add_block(totals, tile, coord, hour_rows)

    totals = jnp.zeros((user_rows, rank), jnp.float32)
    totals = lax.fori_loop(0, count, own_step, totals)
    summed = lax.psum(totals, ("item", "tm"))
    position = lax.axis_index("item") * lax.axis_size("tm") + lax.axis_index("tm")
    mttkrp = lax.dynamic_slice_in_dim(summed, position * share_rows, share_rows, 0)
    gram_items, gram_hours = lax.psum(
        (self_product(item_factor), self_product(hour_factor)), ("user", "item", "tm")
    )
    gram = gram_items * gram_hours
    group = 16

    def sweep(block, factor):
        for offset in range(group):
            factor = update_column(factor, mttkrp, gram, block * group + offset)
        return factor

    return lax.fori_loop(0, rank // group, sweep, a_factor)


def solution(mesh):
    placed = (
        P("user", "item", "tm", None, None, None),
        P("user", "item", "tm", None, None),
        P("user", "item", "tm"),
        P(("user", "item", "tm"), None),
        P(("item", "user", "tm"), None),
        P(("tm", "user", "item"), None),
    )
    return jax.shard_map(
        per_device,
        mesh=mesh,
        in_specs=placed,
        out_specs=P(("user", "item", "tm"), None),
        check_vma=False,
    )
```

profile of v0, /device:TPU:2, one launch (start us, length us, event | category | flops | bytes accessed | tf_op | source)
XLA Modules:
  0.0 590.2 jit_solution(8561335520772189482)
XLA Ops:
  6.5 1.6 fusion.118
  8.1 1.6 fusion.119
  9.8 57.2 %all_gather.6 = bf16[1024,128]{1,0:T(8,128)(2,1)S(1)} all-gather(bf16[8,128]{1,0:T(8,128)(2,1)} %param.14), channel_id=1, replica_groups=mesh['user'=8,'item'=4,'tm'=16] {'user','tm'}, dimensions={0}, use_global_device_ids=true | all-gather | bytes 264192 | tf_op jit(solution)/shard_map/all_gather | solution.py:29
  67.0 41.9 %all_gather.7 = bf16[512,128]{1,0:T(8,128)(2,1)S(1)} all-gather(bf16[16,128]{1,0:T(8,128)(2,1)} %param.15), channel_id=1, replica_groups=mesh['user'=8,'item'=4,'tm'=16] {'user','item'}, dimensions={0}, use_global_device_ids=true | all-gather | bytes 135168 | tf_op jit(solution)/shard_map/all_gather | solution.py:30
  109.6 10.6 %while.26 = (s32[]{:T(128)}, f32[1024,128]{1,0:T(8,128)S(1)}, s32[]{:T(128)}, s32[8,3]{0,1:T(4,128)S(1)}, s32[]{:T(128)}, /*index=5*/bf16[8,64,4096]{2,1,0:T(8,1...) while((s32[]{:T(128)}, f32[1024,128]{1,0:T(8,128)S(1)}, ...), condition=%wide.region_3.4_spmd, body=%wide.region_2.3_spmd.sunk | while | flops 68182032 | bytes 2851221 | solution.py:59
  113.2 1.4 fusion.181
  118.1 1.4 fusion.181
  120.1 1.0 copy.7
  121.3 156.1 %all-reduce.6.cloned.1.call-done = (f32[128,128]{1,0:T(8,128)}, f32[128,128]{1,0:T(8,128)}) async-done(((f32[128,128]{1,0:T(8,128)}, f32[128,128]{1,0:T(8,128)}), (f32[128,128]{1,0:T(8,128)}, f32[128,128]{1,0:T(8,128)})) %all-reduce.6.cloned.1.call-update) | async-done | bytes 131088 | tf_op jit(solution)/shard_map/psum | solution.py:63
  277.4 0.9 mul.78
  278.4 190.9 %all-reduce.4.cloned.1.call-done = f32[1024,128]{0,1:T(8,128)} async-done(((f32[1024,128]{0,1:T(8,128)}), f32[1024,128]{0,1:T(8,128)}) %all-reduce.4.cloned.1.call-update) | async-done | bytes 524304 | tf_op jit(solution)/shard_map/psum | solution.py:60
  469.3 0.9 constant_dynamic-slice_fusion.65
  470.2 112.5 %while.27 = (s32[]{:T(128)}, f32[16,128]{0,1:T(8,128)S(1)}, f32[16,128]{0,1:T(8,128)S(1)}, f32[128,128]{0,1:T(8,128)S(1)}, s32[]{:T(128)}, /*index=5*/s32[]{:T(1...) while((s32[]{:T(128)}, f32[16,128]{0,1:T(8,128)S(1)}, ...), condition=%wide.region_6.7_spmd, body=%wide.region_5.6_spmd.sunk | while | flops 394322 | bytes 1094245 | solution.py:74
  473.5 0.9 fusion.202
  474.4 0.9 fusion.203
  476.1 0.8 fusion.205
  479.3 0.8 fusion.209
  481.0 0.8 fusion.211
  482.6 0.8 fusion.213
  487.6 0.9 fusion.202
  488.5 0.9 fusion.203
  490.1 0.8 fusion.205
  491.8 0.8 fusion.207
  493.4 0.8 fusion.209
  495.0 0.8 fusion.211
  496.7 0.8 fusion.213
  501.7 0.9 fusion.202
  502.6 0.9 fusion.203
  504.2 0.8 fusion.205
  505.8 0.8 fusion.207
  507.4 0.8 fusion.209
  509.1 0.8 fusion.211
  510.8 0.8 fusion.213
  515.7 0.9 fusion.202
  516.6 0.9 fusion.203
  518.3 0.8 fusion.205
  519.9 0.8 fusion.207
  521.5 0.8 fusion.209
  523.2 0.8 fusion.211
  524.8 0.8 fusion.213
  529.8 0.9 fusion.202
  530.7 0.9 fusion.203
  532.3 0.8 fusion.205
  535.6 0.8 fusion.209
  537.2 0.8 fusion.211
  538.9 0.8 fusion.213
  543.9 0.9 fusion.202
  544.8 0.9 fusion.203
  546.4 0.8 fusion.205
  549.6 0.8 fusion.209
  551.3 0.8 fusion.211
  553.0 0.8 fusion.213
  557.9 0.9 fusion.202
  558.8 0.9 fusion.203
  560.4 0.8 fusion.205
  563.7 0.8 fusion.209
  565.4 0.8 fusion.211
  567.0 0.8 fusion.213
  572.0 0.9 fusion.202
  572.9 0.9 fusion.203
  574.5 0.8 fusion.205
  577.8 0.8 fusion.209
  579.4 0.8 fusion.211
  581.1 0.8 fusion.213
  (234 shorter events, 72.0 us)
Async XLA Ops:
  6.5 270.9 %all-reduce.6.cloned.1.call-start = ((), (), s32[]{:S(2)}) async-start(), calls=%async_computation.1 | async-start | bytes 262144 | tf_op jit(solution)/shard_map/psum | solution.py:63
  9.7 459.6 %all-reduce.4.cloned.1.call-start = ((), (), s32[]{:S(2)}) async-start(), calls=%async_computation | async-start | bytes 1048576 | tf_op jit(solution)/shard_map/psum | solution.py:60
  109.6 11.6 %copy-start = (f32[16,128]{1,0:T(8,128)S(1)}, f32[16,128]{1,0:T(8,128)}, u32[]{:S(2)}) copy-start(f32[16,128]{1,0:T(8,128)} %param.13) | copy-start | bytes 24580
Sparse Core Ops, SparseCore 0:
  12.6 264.7 all-reduce.5
  281.3 187.9 all-reduce.3
where the time goes:
time: 592 us; the launch traced here: 590 us
  waiting for transfers between devices  347 us (59%)
  matrix products  107 us (18%)
  blocking collectives  99.1 us (17%)
  local copies, waits for them, and re-layouts  14.5 us (2%)
  between operations  13.5 us (2%)
  loops' own time  7.8 us (1%)
    psum x1, waiting for transfers between devices, per_device(): summed = lax.psum(totals, ('item', 'tm'))  191 us
    psum x1, waiting for transfers between devices, per_device(): lax.psum((self_product(item_factor), self_product(hour_factor)), ('user',...  156 us
    dot_general x128, matrix products, update_column(): fitted = jnp.dot(factor, weights, precision=lax.Precision.HIGHEST)  101 us
    all_gather x1, blocking collectives, per_device(): item_slab = lax.all_gather(item_factor, ('user', 'tm'), axis=0, tiled=True)  57.2 us
    all_gather x1, blocking collectives, per_device(): lax.all_gather(hour_factor, ('user', 'item'), axis=0, tiled=True)  41.9 us
  transfers between devices with their start and end apart: 2, of which 2 were waited for; matrix products, arithmetic and copies ran while one was open for 1% of the time, Pallas kernels for 0%

commit v1 on v0

--- a/solution.py
+++ b/solution.py
@@ -61,7 +61,7 @@
     position = lax.axis_index("item") * lax.axis_size("tm") + lax.axis_index("tm")
     mttkrp = lax.dynamic_slice_in_dim(summed, position * share_rows, share_rows, 0)
     gram_items, gram_hours = lax.psum(
-        (self_product(item_factor), self_product(hour_factor)), ("user", "item", "tm")
+        lax.psum((self_product(item_factor), self_product(hour_factor)), "user"), ("item", "tm")
     )
     gram = gram_items * gram_hours
     group = 16

time: 592 us -> 463 us (0.78)
  the two profiles are of different devices: /device:TPU:2 before, /device:TPU:1 now
where the time goes in v1:
time: 463 us; the launch traced here: 460 us
  waiting for transfers between devices  227 us (49%)
  matrix products  105 us (23%)
  blocking collectives  94.2 us (20%)
  local copies, waits for them, and re-layouts  13.9 us (3%)
  between operations  13.5 us (3%)
  loops' own time  5.11 us (1%)
    psum x1, waiting for transfers between devices, per_device(): summed = lax.psum(totals, ('item', 'tm'))  227 us
    dot_general x128, matrix products, update_column(): fitted = jnp.dot(factor, weights, precision=lax.Precision.HIGHEST)  101 us
    all_gather x1, blocking collectives, per_device(): item_slab = lax.all_gather(item_factor, ('user', 'tm'), axis=0, tiled=True)  58.6 us
    all_gather x1, blocking collectives, per_device(): lax.all_gather(hour_factor, ('user', 'item'), axis=0, tiled=True)  35.6 us
  transfers between devices with their start and end apart: 2, of which 1 were waited for; matrix products, arithmetic and copies ran while one was open for 1% of the time, Pallas kernels for 0%

profile of v1, /device:TPU:1, one launch (start us, length us, event | category | flops | bytes accessed | tf_op | source)
XLA Modules:
  0.0 460.5 jit_solution(378344251121175964)
XLA Ops:
  6.5 1.6 fusion.118
  8.1 1.6 fusion.119
  9.8 58.6 %all_gather.6 = bf16[1024,128]{1,0:T(8,128)(2,1)S(1)} all-gather(bf16[8,128]{1,0:T(8,128)(2,1)} %param.14), channel_id=1, replica_groups=mesh['user'=8,'item'=4,'tm'=16] {'user','tm'}, dimensions={0}, use_global_device_ids=true | all-gather | bytes 264192 | tf_op jit(solution)/shard_map/all_gather | solution.py:29
  68.3 35.6 %all_gather.7 = bf16[512,128]{1,0:T(8,128)(2,1)S(1)} all-gather(bf16[16,128]{1,0:T(8,128)(2,1)} %param.15), channel_id=1, replica_groups=mesh['user'=8,'item'=4,'tm'=16] {'user','item'}, dimensions={0}, use_global_device_ids=true | all-gather | bytes 135168 | tf_op jit(solution)/shard_map/all_gather | solution.py:30
  104.7 5.5 %while.26 = (s32[]{:T(128)}, f32[1024,128]{1,0:T(8,128)S(1)}, s32[]{:T(128)}, s32[8,3]{0,1:T(4,128)S(1)}, s32[]{:T(128)}, /*index=5*/bf16[8,64,4096]{2,1,0:T(8,1...) while((s32[]{:T(128)}, f32[1024,128]{1,0:T(8,128)S(1)}, ...), condition=%wide.region_5.6_spmd, body=%wide.region_4.5_spmd.sunk | while | flops 68182032 | bytes 2851221 | solution.py:59
  108.2 1.4 fusion.181
  110.2 1.0 copy.7
  111.4 227.2 %all-reduce.5.cloned.1.call-done = (f32[1024,128]{0,1:T(8,128)}, f32[128,128]{1,0:T(8,128)}, f32[128,128]{1,0:T(8,128)}) async-done(((f32[1024,128]{0,1:T(8,128)}, f32[128,128]{1,0:T(8,128)}, f32[128,128]{1,0:T(8,128)}), (f32[1024,128]{0,1:T(8,128)}, f32[128,128]{1,0:T(8,128)}, f32[128,128]{1,0:T(8,128)})) %all-reduce.5.cloned.1.call-update) | async-done | bytes 655376 | tf_op jit(solution)/shard_map/psum | solution.py:60
  338.5 0.9 mul.78
  339.5 0.9 constant_dynamic-slice_fusion.65
  340.4 112.5 %while.27 = (s32[]{:T(128)}, f32[16,128]{0,1:T(8,128)S(1)}, f32[16,128]{0,1:T(8,128)S(1)}, f32[128,128]{0,1:T(8,128)S(1)}, s32[]{:T(128)}, /*index=5*/s32[]{:T(1...) while((s32[]{:T(128)}, f32[16,128]{0,1:T(8,128)S(1)}, ...), condition=%wide.region_8.9_spmd, body=%wide.region_7.8_spmd.sunk | while | flops 394322 | bytes 1094245 | solution.py:74
  343.0 0.8 fusion.201
  345.4 0.9 fusion.204
  346.3 0.9 fusion.205
  347.9 0.8 fusion.207
  349.6 0.8 fusion.209
  351.2 0.8 fusion.211
  352.8 0.8 fusion.213
  357.0 0.8 fusion.201
  359.4 0.9 fusion.204
  360.3 0.9 fusion.205
  362.0 0.8 fusion.207
  363.6 0.8 fusion.209
  365.2 0.8 fusion.211
  366.9 0.8 fusion.213
  371.1 0.8 fusion.201
  373.5 0.9 fusion.204
  374.4 0.9 fusion.205
  376.0 0.8 fusion.207
  377.7 0.8 fusion.209
  379.3 0.8 fusion.211
  380.9 0.8 fusion.213
  387.6 0.9 fusion.204
  388.5 0.9 fusion.205
  390.1 0.8 fusion.207
  391.8 0.8 fusion.209
  393.4 0.8 fusion.211
  395.0 0.8 fusion.213
  399.2 0.8 fusion.201
  401.6 0.9 fusion.204
  402.5 0.9 fusion.205
  404.2 0.8 fusion.207
  405.8 0.8 fusion.209
  407.4 0.8 fusion.211
  409.1 0.8 fusion.213
  413.3 0.8 fusion.201
  415.7 0.9 fusion.204
  416.6 0.9 fusion.205
  418.2 0.8 fusion.207
  419.9 0.8 fusion.209
  421.5 0.8 fusion.211
  423.1 0.8 fusion.213
  429.8 0.9 fusion.204
  430.7 0.9 fusion.205
  432.3 0.8 fusion.207
  434.0 0.8 fusion.209
  435.6 0.8 fusion.211
  437.2 0.8 fusion.213
  443.9 0.9 fusion.204
  444.7 0.9 fusion.205
  446.4 0.8 fusion.207
  448.0 0.8 fusion.209
  449.6 0.8 fusion.211
  451.3 0.8 fusion.213
  (228 shorter events, 69.9 us)
Async XLA Ops:
  6.5 104.7 %all-reduce.7.cloned.1.call-start = ((), (), s32[]{:S(2)}) async-start(), calls=%async_computation.1 | async-start | bytes 262144 | tf_op jit(solution)/shard_map/psum | solution.py:64
  9.7 328.8 %all-reduce.5.cloned.1.call-start = ((), (), s32[]{:S(2)}) async-start(), calls=%async_computation | async-start | bytes 1310720 | tf_op jit(solution)/shard_map/psum | solution.py:60
  104.7 6.6 %copy-start = (f32[16,128]{1,0:T(8,128)S(1)}, f32[16,128]{1,0:T(8,128)}, u32[]{:S(2)}) copy-start(f32[16,128]{1,0:T(8,128)} %param.13) | copy-start | bytes 24580
Sparse Core Ops, SparseCore 0:
  9.8 79.3 all-reduce.6
  111.4 227.1 all-reduce.4
